TPU v7x, 512 devices: a whole 4x8x8 slice. The times are simulated.
512 devices in a mesh: tm: 64 (over y, x, z_lo), run: 8 (over z_hi, core).
Axes of the slice: x: 4, y: 8, z: 8 (z_hi: 4, z_lo: 2; z = z_hi * 2 + z_lo), core: 2. Of those that a mesh axis runs over, the one named last changes fastest.
Arguments:
- signal: bfloat16 [8, 65536, 256], P('run', 'tm'), may hold values from -6 to 6
- conv_weight: bfloat16 [768, 512], replicated, may hold values from -0.21875 to 0.21875
- conv_bias: float32 [512], replicated, may hold values from -3 to 3
- out_weight: bfloat16 [256, 256], replicated, may hold values from -0.375 to 0.375
- out_bias: float32 [256], replicated, may hold values from -3 to 3
- cotangent: bfloat16 [8, 65536, 256], P('run', 'tm'), may hold values from -8 to 8
Outputs:
- output: bfloat16 [8, 65536, 256], P('run', 'tm')
- grad_signal: bfloat16 [8, 65536, 256], P('run', 'tm')
- grad_conv_weight: float32 [768, 512], replicated
- grad_conv_bias: float32 [512], replicated
- grad_out_weight: float32 [256, 256], replicated
- grad_out_bias: float32 [256], replicated
All inputs are finite; a program needn't handle non-finite values.
Results may differ from a plain program's by a relative error of at most 0.0034.
Values may be sent and summed in bfloat16 or wider, within the bound.
A program may use at most 64 MiB of HBM per device.

v0:
```python
import jax
import jax.numpy as jnp
from jax import lax
from jax.sharding import PartitionSpec as P

DILATION_STEPS = 256
KERNEL_TAPS = 3


def passed_along(array, axis, by):
    size = lax.axis_size(axis)
    pairs = [(i, i + by) for i in range(size) if 0 <= i + by < size]
    return lax.ppermute(array, axis, pairs)


def local(signal, conv_weight, conv_bias, out_weight, out_bias, cotangent):
    device_rows = signal.shape[1]
    channels = signal.shape[2]
    receptive_span = (KERNEL_TAPS - 1) * DILATION_STEPS
    history = passed_along(signal[:, device_rows - receptive_span :, :], "tm", 1)
    padded_input = jnp.concatenate([history, signal], 1)
    tap_stack = jnp.concatenate(
        [
            padded_input[
                :,
                receptive_span
                - kernel_tap_index * DILATION_STEPS : receptive_span
                - kernel_tap_index * DILATION_STEPS
                + device_rows,
            ]
            for kernel_tap_index in range(KERNEL_TAPS)
        ],
        2,
    )
    preact = (
        jnp.einsum("bsk,kn->bsn", tap_stack, conv_weight, preferred_element_type=jnp.float32)
        + conv_bias
    )
    filtered = jnp.tanh(preact[..., :channels])
    gated = jax.nn.sigmoid(preact[..., channels:])
    mixed = (filtered * gated).astype(jnp.bfloat16)
    hidden = (
        jnp.einsum("bsc,cd->bsd", mixed, out_weight, preferred_element_type=jnp.float32) + out_bias
    )
    output = (signal.astype(jnp.float32) + hidden).astype(jnp.bfloat16)
    dmixed = jnp.einsum("bsd,cd->bsc", cotangent, out_weight, preferred_element_type=jnp.float32)
    dpre = jnp.concatenate(
        [dmixed * gated * (1.0 - filtered * filtered), dmixed * filtered * gated * (1.0 - gated)], 2
    ).astype(jnp.bfloat16)
    dstacked = jnp.einsum("bsn,kn->bsk", dpre, conv_weight, preferred_element_type=jnp.float32)
    local_grad = jnp.zeros((signal.shape[0], receptive_span + device_rows, channels), jnp.float32)
    for kernel_tap_index in range(KERNEL_TAPS):
        shifted_slice = dstacked[
            ..., kernel_tap_index * channels : (kernel_tap_index + 1) * channels
        ]
        local_grad = local_grad + jnp.pad(
            shifted_slice,
            (
                (0, 0),
                (
                    receptive_span - kernel_tap_index * DILATION_STEPS,
                    kernel_tap_index * DILATION_STEPS,
                ),
                (0, 0),
            ),
        )
    incoming = passed_along(local_grad[:, :receptive_span].astype(jnp.bfloat16), "tm", -1).astype(
        jnp.float32
    )
    grad_signal = (
        cotangent.astype(jnp.float32)
        + local_grad[:, receptive_span:]
        + jnp.pad(incoming, ((0, 0), (device_rows - receptive_span, 0), (0, 0)))
    )
    grad_signal = grad_signal.astype(jnp.bfloat16)
    grad_conv = jnp.einsum("bsk,bsn->kn", tap_stack, dpre, preferred_element_type=jnp.float32)
    grad_cbias = jnp.sum(dpre.astype(jnp.float32), (0, 1))
    grad_proj = jnp.einsum("bsc,bsd->cd", mixed, cotangent, preferred_element_type=jnp.float32)
    grad_pbias = jnp.sum(cotangent.astype(jnp.float32), (0, 1))
    scale = float(signal.shape[0] * lax.axis_size("run") * device_rows * lax.axis_size("tm")) ** (
        -0.5
    )
    summed = lax.psum((grad_conv, grad_cbias, grad_proj, grad_pbias), ("tm", "run"))
    return (
        output,
        grad_signal,
        summed[0] * scale,
        summed[1] * scale,
        summed[2] * scale,
        summed[3] * scale,
    )


def solution(mesh):
    placed = (P("run", "tm", None), P(), P(), P(), P(), P("run", "tm", None))
    return jax.shard_map(
        local,
        mesh=mesh,
        in_specs=placed,
        out_specs=(P("run", "tm", None), P("run", "tm", None), P(), P(), P(), P()),
        check_vma=False,
    )
```

profile of v0, /device:TPU:1, one launch (start us, length us, event | category | flops | bytes accessed | tf_op | source)
XLA Modules:
  0.0 329.9 jit_solution(11281328637928422365)
XLA Ops:
  7.2 1.1 slice.31
  8.3 4.8 %collective-permute-start = (bf16[1,512,256]{2,1,0:T(8,128)(2,1)S(1)}, bf16[1,512,256]{2,1,0:T(8,128)(2,1)S(1)}, u32[]{:S(2)}, u32[]{:S(2)}) collective-permute-start(bf16[1,512,256]{2,1,0:T(8,128)(2,1)S(1)} %slice.31), channel_id=1, source_target_pairs={{0,8},{8,16},{16,24},{24,32},{32,40},{40,48},{48,56},{56,64},{64,7... | collective-permute-start | bytes 786440 | tf_op jit(solution)/shard_map/ppermute | solution.py:13
  13.2 3.3 collective-permute-done
  16.5 1.1 constant_dynamic-update-slice_fusion
  17.5 0.1 fusion.17
  17.7 1.0 add_bitcast_fusion
  18.7 0.8 multiply_convert_fusion.1
  19.5 0.2 convert_reduce_fusion
  19.8 2.2 fusion.8
  21.9 2.7 convolution_bitcast_fusion
  24.6 1.0 fusion.10
  25.6 2.1 fusion.16
  27.7 0.2 pad_add_fusion
  27.9 0.7 slice.74
  28.7 1.3 collective-permute-start.1
  30.0 2.2 fusion.2
  32.2 4.4 %collective-permute-done.1 = bf16[1,512,256]{2,1,0:T(8,128)(2,1)} collective-permute-done((bf16[1,512,256]{2,1,0:T(8,128)(2,1)}, bf16[1,512,256]{2,1,0:T(8,128)(2,1)}, u32[]{:S(2)}, u32[]{:S(2)}) %collective-permute-start.1) | collective-permute-done | bytes 262176 | tf_op jit(solution)/shard_map/ppermute | solution.py:13
  36.6 2.0 convert_reduce_fusion.1
  38.6 113.1 %all-reduce.4 = (f32[512]{0:T(512)S(1)}, f32[256]{0:T(256)S(1)}) all-reduce(f32[512]{0:T(512)S(1)} %convert_reduce_fusion, f32[256]{0:T(256)S(1)} %get-tuple-element.18), channel_id=1, replica_groups=mesh['tm'=64,'run'=8] {'tm','run'}, use_global_device_ids=true, to_apply=%region_2.3 | all-reduce | flops 768 | bytes 6144 | tf_op jit(solution)/shard_map/psum | solution.py:83
  151.6 0.6 broadcast_multiply_fusion.3
  152.2 0.6 broadcast_multiply_fusion.2
  152.8 166.8 %all-reduce.8.cloned.1.call-done = (f32[768,512]{1,0:T(8,128)}, f32[256,256]{1,0:T(8,128)}) async-done(((f32[768,512]{1,0:T(8,128)}, f32[256,256]{1,0:T(8,128)}), (f32[768,512]{1,0:T(8,128)}, f32[256,256]{1,0:T(8,128)})) %all-reduce.8.cloned.1.call-update) | async-done | bytes 1835024 | tf_op jit(solution)/shard_map/psum | solution.py:83
  319.5 2.8 broadcast_multiply_fusion
  322.3 0.7 broadcast_multiply_fusion.1
  (19 shorter events, 0.1 us)
Async XLA Ops:
  7.2 10.5 %copy-start = (bf16[768,512]{1,0:T(8,128)(2,1)S(1)}, bf16[768,512]{1,0:T(8,128)(2,1)}, u32[]{:S(2)}) copy-start(bf16[768,512]{1,0:T(8,128)(2,1)} %param.7) | copy-start | bytes 2359300
  7.2 10.5 %copy-start.2 = (bf16[1,1024,256]{2,1,0:T(8,128)(2,1)S(1)}, bf16[1,1024,256]{2,1,0:T(8,128)(2,1)}, u32[]{:S(2)}) copy-start(bf16[1,1024,256]{2,1,0:T(8,128)(2,1)} %param.6) | copy-start | bytes 1572868
  7.2 10.5 %copy-start.6 = (f32[512]{0:T(512)S(1)}, f32[512]{0:T(512)}, u32[]{:S(2)}) copy-start(f32[512]{0:T(512)} %param.8) | copy-start | bytes 6148
  7.2 312.3 %all-reduce.8.cloned.1.call-start = ((), (), s32[]{:S(2)}) async-start(), calls=%async_computation | async-start | bytes 3670016 | tf_op jit(solution)/shard_map/psum | solution.py:83
  8.3 8.1 %collective-permute-start = (bf16[1,512,256]{2,1,0:T(8,128)(2,1)S(1)}, bf16[1,512,256]{2,1,0:T(8,128)(2,1)S(1)}, u32[]{:S(2)}, u32[]{:S(2)}) collective-permute-start(bf16[1,512,256]{2,1,0:T(8,128)(2,1)S(1)} %slice.31), channel_id=1, source_target_pairs={{0,8},{8,16},{16,24},{24,32},{32,40},{40,48},{48,56},{56,64},{64,7... | collective-permute-start | bytes 786440 | tf_op jit(solution)/shard_map/ppermute | solution.py:13
  17.7 1.1 copy-start.1
  17.7 1.1 copy-start.5
  19.5 5.1 %copy-start.3 = (bf16[1024,256]{0,1:T(8,128)(2,1)}, bf16[1024,256]{0,1:T(8,128)(2,1)S(1)}, u32[]{:S(2)}) copy-start(bf16[1024,256]{0,1:T(8,128)(2,1)S(1)} %get-tuple-element.15) | copy-start | bytes 1572868
  27.9 2.1 copy-start.7
  28.7 7.9 %collective-permute-start.1 = (bf16[1,512,256]{2,1,0:T(8,128)(2,1)}, bf16[1,512,256]{2,1,0:T(8,128)(2,1)}, u32[]{:S(2)}, u32[]{:S(2)}) collective-permute-start(bf16[1,512,256]{2,1,0:T(8,128)(2,1)} %slice.74), channel_id=1, source_target_pairs={{8,0},{16,8},{24,16},{32,24},{40,32},{48,40},{56,48},{64,56},{72,6... | collective-permute-start | bytes 786440 | tf_op jit(solution)/shard_map/ppermute | solution.py:13
  319.5 2.8 copy-start.4
Sparse Core Ops, SparseCore 0:
  30.1 289.3 all-reduce.7
where the time goes:
time: 330 us
  waiting for transfers between devices  174 us (53%)
  blocking collectives  113 us (34%)
  between operations  14.2 us (4%)
  matrix products  9.89 us (3%)
  other arithmetic  7.02 us (2%)
  starting transfers between devices  6.16 us (2%)
  local copies, waits for them, and re-layouts  5.08 us (2%)
    psum x1, waiting for transfers between devices, local(): lax.psum((grad_conv, grad_cbias, grad_proj, grad_pbias), ('tm', 'run'))  167 us
    psum x1, blocking collectives, local(): lax.psum((grad_conv, grad_cbias, grad_proj, grad_pbias), ('tm', 'run'))  113 us
    ppermute x2, waiting for transfers between devices, passed_along(): return lax.ppermute(array, axis, pairs)  7.68 us
  transfers between devices with their start and end apart: 3, of which 3 were waited for; matrix products, arithmetic and copies ran while one was open for 2% of the time, Pallas kernels for 0%

commit v1 on v0

--- a/solution.py
+++ b/solution.py
@@ -80,7 +80,7 @@
     scale = float(signal.shape[0] * lax.axis_size("run") * device_rows * lax.axis_size("tm")) ** (
         -0.5
     )
-    summed = lax.psum((grad_conv, grad_cbias, grad_proj, grad_pbias), ("tm", "run"))
+    summed = lax.psum(lax.psum((grad_conv, grad_cbias, grad_proj, grad_pbias), "run"), "tm")
     return (
         output,
         grad_signal,

time: 330 us -> 738 us (2.24)
  the two profiles are of different devices: /device:TPU:1 before, /device:TPU:30 now
where the time goes in v1:
time: 738 us
  waiting for transfers between devices  530 us (72%)
  blocking collectives  171 us (23%)
  between operations  14.2 us (2%)
  starting transfers between devices  7.53 us (1%)
    psum x1, waiting for transfers between devices, local(): lax.psum(lax.psum((grad_conv, grad_cbias, grad_proj, grad_pbias), 'run'),...  424 us
    psum x1, blocking collectives, local(): lax.psum(lax.psum((grad_conv, grad_cbias, grad_proj, grad_pbias), 'run'),...  154 us
    psum x1, waiting for transfers between devices, local(): lax.psum((grad_conv, grad_cbias, grad_proj, grad_pbias), 'run')  94.2 us
    psum x1, blocking collectives, local(): lax.psum((grad_conv, grad_cbias, grad_proj, grad_pbias), 'run')  16.2 us
  transfers between devices with their start and end apart: 4, of which 4 were waited for; matrix products, arithmetic and copies ran while one was open for 1% of the time, Pallas kernels for 0%

profile of v1, /device:TPU:30, one launch (start us, length us, event | category | flops | bytes accessed | tf_op | source)
XLA Modules:
  0.0 738.0 jit_solution(1374340505601241953)
XLA Ops:
  7.3 1.1 slice.31
  8.3 4.3 collective-permute-start
  12.6 6.6 collective-permute-done
  19.2 1.1 constant_dynamic-update-slice_fusion
  20.4 1.0 add_bitcast_fusion
  21.5 0.8 multiply_convert_fusion.1
  22.2 1.0 fusion.10
  23.2 2.2 fusion.8
  25.5 94.2 %all-reduce.13.cloned.1.call-done = (f32[768,512]{1,0:T(8,128)}, f32[256,256]{1,0:T(8,128)}) async-done(((f32[768,512]{1,0:T(8,128)}, f32[256,256]{1,0:T(8,128)}), (f32[768,512]{1,0:T(8,128)}, f32[256,256]{1,0:T(8,128)})) %all-reduce.13.cloned.1.call-update) | async-done | bytes 1835024 | tf_op jit(solution)/shard_map/psum | solution.py:83
  119.7 1.0 convolution_bitcast_fusion
  120.8 0.3 fusion.16
  121.1 0.2 pad_add_fusion
  121.4 3.2 collective-permute-start.1
  124.5 0.2 convert_reduce_fusion
  124.8 1.2 fusion.2
  125.9 4.4 collective-permute-done.1
  130.3 1.1 convert_reduce_fusion.1
  131.4 16.2 %all-reduce.6 = (f32[512]{0:T(512)S(1)}, f32[256]{0:T(256)S(1)}) all-reduce(f32[512]{0:T(512)S(1)} %convert_reduce_fusion, f32[256]{0:T(256)S(1)} %get-tuple-element.22), channel_id=1, replica_groups=mesh['tm'=64,'run'=8] {'run'}, use_global_device_ids=true, to_apply=%region_3.4 | all-reduce | flops 768 | bytes 6144 | tf_op jit(solution)/shard_map/psum | solution.py:83
  147.6 154.5 %all-reduce.4 = (f32[512]{0:T(512)S(1)}, f32[256]{0:T(256)S(1)}) all-reduce(f32[512]{0:T(512)S(1)} %get-tuple-element.10, f32[256]{0:T(256)S(1)} %get-tuple-element.11), channel_id=1, replica_groups=mesh['tm'=64,'run'=8] {'tm'}, use_global_device_ids=true, to_apply=%region_4.5 | all-reduce | flops 768 | bytes 6144 | tf_op jit(solution)/shard_map/psum | solution.py:83
  302.1 0.6 broadcast_multiply_fusion.3
  302.7 0.6 broadcast_multiply_fusion.2
  303.2 424.4 %all-reduce.11.cloned.1.call-done = (f32[768,512]{1,0:T(8,128)}, f32[256,256]{1,0:T(8,128)}) async-done(((f32[768,512]{1,0:T(8,128)}, f32[256,256]{1,0:T(8,128)}), (f32[768,512]{1,0:T(8,128)}, f32[256,256]{1,0:T(8,128)})) %all-reduce.11.cloned.1.call-update) | async-done | bytes 1835024 | tf_op jit(solution)/shard_map/psum | solution.py:83
  727.7 2.8 broadcast_multiply_fusion
  730.4 0.7 broadcast_multiply_fusion.1
  (21 shorter events, 0.3 us)
Async XLA Ops:
  7.2 13.2 %copy-start = (bf16[768,512]{1,0:T(8,128)(2,1)S(1)}, bf16[768,512]{1,0:T(8,128)(2,1)}, u32[]{:S(2)}) copy-start(bf16[768,512]{1,0:T(8,128)(2,1)} %param.7) | copy-start | bytes 2359300
  7.2 13.2 %copy-start.2 = (bf16[1,1024,256]{2,1,0:T(8,128)(2,1)S(1)}, bf16[1,1024,256]{2,1,0:T(8,128)(2,1)}, u32[]{:S(2)}) copy-start(bf16[1,1024,256]{2,1,0:T(8,128)(2,1)} %param.6) | copy-start | bytes 1572868
  7.2 13.2 %copy-start.5 = (f32[512]{0:T(512)S(1)}, f32[512]{0:T(512)}, u32[]{:S(2)}) copy-start(f32[512]{0:T(512)} %param.8) | copy-start | bytes 6148
  7.2 112.5 %all-reduce.13.cloned.1.call-start = ((), (), s32[]{:S(2)}) async-start(), calls=%async_computation.1 | async-start | bytes 3670016 | tf_op jit(solution)/shard_map/psum | solution.py:83
  8.3 10.8 %collective-permute-start = (bf16[1,512,256]{2,1,0:T(8,128)(2,1)S(1)}, bf16[1,512,256]{2,1,0:T(8,128)(2,1)S(1)}, u32[]{:S(2)}, u32[]{:S(2)}) collective-permute-start(bf16[1,512,256]{2,1,0:T(8,128)(2,1)S(1)} %slice.31), channel_id=1, source_target_pairs={{0,8},{8,16},{16,24},{24,32},{32,40},{40,48},{48,56},{56,64},{64,7... | collective-permute-start | bytes 786440 | tf_op jit(solution)/shard_map/ppermute | solution.py:13
  20.4 1.1 copy-start.1
  20.4 1.1 copy-start.4
  25.4 702.2 %all-reduce.11.cloned.1.call-start = ((), (), s32[]{:S(2)}) async-start(), calls=%async_computation | async-start | bytes 3670016 | tf_op jit(solution)/shard_map/psum | solution.py:83
  121.1 3.7 copy-start.6
  121.4 9.0 %collective-permute-start.1 = (bf16[1,512,256]{2,1,0:T(8,128)(2,1)S(1)}, bf16[1,512,256]{2,1,0:T(8,128)(2,1)S(1)}, u32[]{:S(2)}, u32[]{:S(2)}) collective-permute-start(bf16[1,512,256]{2,1,0:T(8,128)(2,1)S(1)} %slice.74), channel_id=1, source_target_pairs={{8,0},{16,8},{24,16},{32,24},{40,32},{48,40},{56,48},{64,56},{72,6... | collective-permute-start | bytes 786440 | tf_op jit(solution)/shard_map/ppermute | solution.py:13
  727.7 2.8 copy-start.3
Sparse Core Ops, SparseCore 0:
  25.6 94.0 all-reduce.12
  122.7 604.9 all-reduce.10
